TPU v7x, 32 devices: a whole 2x2x4 slice. The times are simulated.
32 devices in a mesh: pair: 2 (over x), blk: 8 (over z, y), group: 2 (over core).
Axes of the slice: x: 2, y: 2, z: 4, core: 2. Of those that a mesh axis runs over, the one named last changes fastest.
Arguments:
- codes: int32 [32, 1536, 256], P(('pair', 'blk', 'group')), may hold values from 0 to 255
- scales: int32 [32, 1536, 8], P(('pair', 'blk', 'group')), may hold values from -7 to 0
- inputs: bfloat16 [4096, 1536], P(('pair', 'blk', 'group')), may hold values from -6 to 6
- cotangent: bfloat16 [4096, 256], P(('pair', 'blk', 'group')), may hold values from -6 to 6
Outputs:
- earlier_grad: float32 [1536, 256], replicated
- current_grad: float32 [1536, 256], replicated
All inputs are finite; a program needn't handle non-finite values.
Results may differ from a plain program's by a relative error of at most 0.0003.
Values sent between devices are 32-bit elements; how exact they have to be, the bound alone decides.
No kernel may reach another device: no remote copies, remote signals or barrier semaphores. Data moves between devices by JAX's collectives and lax.ppermute only.
A program may use at most 64 MiB of HBM per device.

v0:
```python
import jax
import jax.numpy as jnp
from jax import lax
from jax.sharding import PartitionSpec as P


def decode(codes, scales):
    codes = codes[0]
    scales = scales[0]
    rows, width = codes.shape
    sign = 1.0 - 2.0 * (codes // 128).astype(jnp.float32)
    field = codes // 8 % 16
    mant = (codes % 8).astype(jnp.float32)
    frac = jnp.where(field > 0, 8.0 + mant, mant)
    power = jnp.where(field > 0, field, 1) - 10
    expo = power.reshape(rows, scales.shape[1], width // scales.shape[1]) + scales[:, :, None]
    return sign * frac * jnp.exp2(expo.reshape(rows, width).astype(jnp.float32))


def combine(stack, count):
    pooled = lax.psum(stack, "pair")
    share = lax.psum_scatter(pooled, "blk", scatter_dimension=1, tiled=True)
    total = lax.psum_scatter(share, "group", scatter_dimension=1, tiled=True) / count
    return lax.all_gather(total, ("blk", "group"), axis=1, tiled=True)


def key_product(inputs, cotangent):
    return lax.dot_general(
        inputs, cotangent, (((0,), (0,)), ((), ())), preferred_element_type=jnp.float32
    )


def local(codes, scales, inputs, cotangent):
    count = lax.axis_size("pair") * lax.axis_size("blk") * lax.axis_size("group")
    decoded = decode(codes, scales)
    product = key_product(inputs, cotangent)
    summed = combine(jnp.stack([decoded, product]), count)
    earlier_grad = summed[0]
    current_grad = summed[1]
    return (earlier_grad, current_grad)


def solution(mesh):
    in_specs = (
        P(("pair", "blk", "group"), None, None),
        P(("pair", "blk", "group"), None, None),
        P(("pair", "blk", "group"), None),
        P(("pair", "blk", "group"), None),
    )
    out_specs = (P(), P())
    return jax.shard_map(local, mesh=mesh, in_specs=in_specs, out_specs=out_specs, check_vma=False)
```

profile of v0, /device:TPU:0, one launch (start us, length us, event | category | flops | bytes accessed | tf_op | source)
XLA Modules:
  0.0 186.2 jit_solution(1373778970033017761)
XLA Ops:
  7.2 0.0 copy-start
  7.2 0.0 reduce-scatter.3.cloned.1.call-start
  7.2 1.0 add.58
  8.2 0.5 copy.7
  8.7 0.0 copy-start.1
  8.7 4.5 %fusion.5 = f32[1,1536,256]{2,1,0:T(8,128)S(1)} fusion(s32[1,1536,256]{2,1,0:T(8,128)S(1)} %copy.7, s32[1,1536,256]{2,1,0:T(8,128)} %param.4), kind=kLoop, calls=%fused_computation.20 | loop fusion | flops 21233664 | bytes 4718592 | tf_op jit(solution)/shard_map/mul | solution.py:17
  13.2 0.0 copy-done
  13.2 0.0 copy-done.1
  13.3 0.4 convolution_bitcast_fusion
  13.6 1.9 pad_maximum_fusion
  15.5 0.0 reduce-scatter.3.cloned.1.call-update
  15.5 0.0 reduce-scatter.5.cloned.1.call-start
  15.6 77.1 %reduce-scatter.3.cloned.1.call-done = f32[2,192,256]{2,1,0:T(8,128)} async-done(((f32[2,1536,256]{2,1,0:T(8,128)}), f32[2,192,256]{2,1,0:T(8,128)}) %reduce-scatter.3.cloned.1.call-update) | async-done | bytes 393232 | tf_op jit(solution)/shard_map/reduce_scatter | solution.py:22
  92.7 0.0 reduce-scatter.5.cloned.1.call-update
  92.7 0.0 all-reduce.2.cloned.1.call-start
  92.8 9.1 %reduce-scatter.5.cloned.1.call-done = f32[2,96,256]{2,1,0:T(8,128)} async-done(((f32[2,192,256]{2,1,0:T(8,128)}), f32[2,96,256]{2,1,0:T(8,128)}) %reduce-scatter.5.cloned.1.call-update) | async-done | bytes 196624 | tf_op jit(solution)/shard_map/reduce_scatter | solution.py:23
  101.9 0.0 all-reduce.2.cloned.1.call-update
  101.9 0.0 all-gather.2.cloned.1.call-start
  102.0 25.8 %all-reduce.2.cloned.1.call-done = f32[2,96,256]{2,1,0:T(8,128)} async-done(((f32[2,96,256]{2,1,0:T(8,128)}), f32[2,96,256]{2,1,0:T(8,128)}) %all-reduce.2.cloned.1.call-update) | async-done | bytes 196624 | tf_op jit(solution)/shard_map/psum | solution.py:21
  127.7 1.6 broadcast_multiply_fusion
  129.3 0.0 all-gather.2.cloned.1.call-update
  129.4 46.6 %all-gather.2.cloned.1.call-done = f32[2,1536,256]{2,1,0:T(8,128)} async-done(((f32[2,96,256]{2,1,0:T(8,128)}), f32[2,1536,256]{2,1,0:T(8,128)}) %all-gather.2.cloned.1.call-update) | async-done | bytes 3145744 | tf_op jit(solution)/shard_map/all_gather | solution.py:24
  176.0 3.7 %slice_bitcast_fusion = (f32[1536,256]{1,0:T(8,128)}, f32[1536,256]{1,0:T(8,128)}) fusion(f32[2,1536,256]{2,1,0:T(8,128)} %all-gather.2.cloned.1.call-done), kind=kLoop, calls=%fused_computation.28 | loop fusion | bytes 6291456 | tf_op jit(solution)/shard_map/squeeze | solution.py:39
Async XLA Ops:
  7.2 6.1 %copy-start = (bf16[128,1536]{1,0:T(8,128)(2,1)S(1)}, bf16[128,1536]{1,0:T(8,128)(2,1)}, u32[]{:S(2)}) copy-start(bf16[128,1536]{1,0:T(8,128)(2,1)} %param.6) | copy-start | bytes 1179652
  7.2 85.5 %reduce-scatter.3.cloned.1.call-start = ((), (), s32[]{:S(2)}) async-start(), calls=%async_computation.3 | async-start | bytes 3538944 | tf_op jit(solution)/shard_map/reduce_scatter | solution.py:22
  8.7 4.5 %copy-start.1 = (bf16[128,256]{1,0:T(8,128)(2,1)S(1)}, bf16[128,256]{1,0:T(8,128)(2,1)}, u32[]{:S(2)}) copy-start(bf16[128,256]{1,0:T(8,128)(2,1)} %param.7) | copy-start | bytes 196612
  15.5 86.4 %reduce-scatter.5.cloned.1.call-start = ((), (), s32[]{:S(2)}) async-start(), calls=%async_computation.4 | async-start | bytes 589824 | tf_op jit(solution)/shard_map/reduce_scatter | solution.py:23
  92.7 35.0 %all-reduce.2.cloned.1.call-start = ((), (), s32[]{:S(2)}) async-start(), calls=%async_computation.5 | async-start | bytes 393216 | tf_op jit(solution)/shard_map/psum | solution.py:21
  101.9 74.0 %all-gather.2.cloned.1.call-start = ((), (), s32[]{:S(2)}) async-start(), calls=%async_computation.2 | async-start | bytes 3342336 | tf_op jit(solution)/shard_map/all_gather | solution.py:24
Sparse Core Ops, SparseCore 0:
  15.7 77.0 reduce-scatter.2
  94.9 6.8 reduce-scatter.4
  104.2 23.5 all-reduce.1
  130.4 45.4 all-gather.1
where the time goes:
time: 186 us
  waiting for transfers between devices  159 us (85%)
  between operations  13.8 us (7%)
  other arithmetic  7.97 us (4%)
  local copies, waits for them, and re-layouts  5.23 us (3%)
    reduce_scatter x1, waiting for transfers between devices, combine(): share = lax.psum_scatter(pooled, 'blk', scatter_dimension=1, tiled=True)  77.1 us
    all_gather x1, waiting for transfers between devices, combine(): return lax.all_gather(total, ('blk', 'group'), axis=1, tiled=True)  46.6 us
    psum x1, waiting for transfers between devices, combine(): pooled = lax.psum(stack, 'pair')  25.8 us
    reduce_scatter x1, waiting for transfers between devices, combine(): lax.psum_scatter(share, 'group', scatter_dimension=1, tiled=True) / count  9.11 us
    mul x1, other arithmetic, decode(): return sign * frac * jnp.exp2(expo.reshape(rows, width).astype(jnp.float32))  4.5 us
    squeeze x1, local copies, waits for them, and re-layouts, local(): current_grad = summed[1]  3.74 us
  transfers between devices with their start and end apart: 4, of which 4 were waited for; matrix products, arithmetic and copies ran while one was open for 0% of the time, Pallas kernels for 0%

commit v1 on v0

--- a/solution.py
+++ b/solution.py
@@ -2,6 +2,7 @@
 import jax.numpy as jnp
 from jax import lax
 from jax.sharding import PartitionSpec as P
+from jax.lax import all_gather
 
 
 def decode(codes, scales):
@@ -21,7 +22,8 @@
     pooled = lax.psum(stack, "pair")
     share = lax.psum_scatter(pooled, "blk", scatter_dimension=1, tiled=True)
     total = lax.psum_scatter(share, "group", scatter_dimension=1, tiled=True) / count
-    return lax.all_gather(total, ("blk", "group"), axis=1, tiled=True)
+    refer_the_knots = lambda t0: jnp.concatenate(all_gather(t0, ("blk", "group")), 1)
+    return refer_the_knots(total)
 
 
 def key_product(inputs, cotangent):

time: 186 us -> 187 us (level)
    slice x0 -> x1, local copies, waits for them, and re-layouts: none -> 3.87 us  [local(): current_grad = summed[1]]
    squeeze x1 -> x0, local copies, waits for them, and re-layouts: 3.74 us -> none  [local(): current_grad = summed[1]]
where the time goes in v1:
time: 187 us; the launch traced here: 186 us
  waiting for transfers between devices  159 us (85%)
  between operations  13.8 us (7%)
  other arithmetic  7.97 us (4%)
  local copies, waits for them, and re-layouts  5.36 us (3%)
    reduce_scatter x1, waiting for transfers between devices, combine(): share = lax.psum_scatter(pooled, 'blk', scatter_dimension=1, tiled=True)  77.1 us
    all_gather x1, waiting for transfers between devices, combine(): all_gather(t0, ('blk', 'group'))  46.5 us
    psum x1, waiting for transfers between devices, combine(): pooled = lax.psum(stack, 'pair')  25.8 us
    reduce_scatter x1, waiting for transfers between devices, combine(): lax.psum_scatter(share, 'group', scatter_dimension=1, tiled=True) / count  9.11 us
    mul x1, other arithmetic, decode(): return sign * frac * jnp.exp2(expo.reshape(rows, width).astype(jnp.float32))  4.5 us
    slice x1, local copies, waits for them, and re-layouts, local(): current_grad = summed[1]  3.87 us
  transfers between devices with their start and end apart: 4, of which 4 were waited for; matrix products, arithmetic and copies ran while one was open for 0% of the time, Pallas kernels for 0%

profile of v1, /device:TPU:0, one launch (start us, length us, event | category | flops | bytes accessed | tf_op | source)
XLA Modules:
  0.0 186.3 jit_solution(7870009971666345618)
XLA Ops:
  7.2 0.0 copy-start
  7.2 0.0 reduce-scatter.3.cloned.1.call-start
  7.2 1.0 add.58
  8.2 0.5 copy.8
  8.7 0.0 copy-start.1
  8.7 4.5 %fusion.5 = f32[1,1536,256]{2,1,0:T(8,128)S(1)} fusion(s32[1,1536,256]{2,1,0:T(8,128)S(1)} %copy.8, s32[1,1536,256]{2,1,0:T(8,128)} %param.4), kind=kLoop, calls=%fused_computation.20 | loop fusion | flops 21233664 | bytes 4718592 | tf_op jit(solution)/shard_map/mul | solution.py:18
  13.2 0.0 copy-done
  13.2 0.0 copy-done.1
  13.3 0.4 convolution_bitcast_fusion
  13.6 1.9 pad_maximum_fusion
  15.5 0.0 reduce-scatter.3.cloned.1.call-update
  15.5 0.0 reduce-scatter.5.cloned.1.call-start
  15.6 77.1 %reduce-scatter.3.cloned.1.call-done = f32[2,192,256]{2,1,0:T(8,128)} async-done(((f32[2,1536,256]{2,1,0:T(8,128)}), f32[2,192,256]{2,1,0:T(8,128)}) %reduce-scatter.3.cloned.1.call-update) | async-done | bytes 393232 | tf_op jit(solution)/shard_map/reduce_scatter | solution.py:23
  92.7 0.0 reduce-scatter.5.cloned.1.call-update
  92.7 0.0 all-reduce.2.cloned.1.call-start
  92.8 9.1 %reduce-scatter.5.cloned.1.call-done = f32[2,96,256]{2,1,0:T(8,128)} async-done(((f32[2,192,256]{2,1,0:T(8,128)}), f32[2,96,256]{2,1,0:T(8,128)}) %reduce-scatter.5.cloned.1.call-update) | async-done | bytes 196624 | tf_op jit(solution)/shard_map/reduce_scatter | solution.py:24
  101.9 0.0 all-reduce.2.cloned.1.call-update
  101.9 0.0 all-gather.3.cloned.1.call-start
  102.0 25.8 %all-reduce.2.cloned.1.call-done = f32[2,96,256]{2,1,0:T(8,128)} async-done(((f32[2,96,256]{2,1,0:T(8,128)}), f32[2,96,256]{2,1,0:T(8,128)}) %all-reduce.2.cloned.1.call-update) | async-done | bytes 196624 | tf_op jit(solution)/shard_map/psum | solution.py:22
  127.7 1.6 broadcast_multiply_fusion
  129.3 0.0 all-gather.3.cloned.1.call-update
  129.4 46.5 %all-gather.3.cloned.1.call-done = f32[32,96,256]{2,1,0:T(8,128)} async-done(((f32[2,96,256]{2,1,0:T(8,128)}), f32[32,96,256]{2,1,0:T(8,128)}) %all-gather.3.cloned.1.call-update) | async-done | bytes 3145744 | tf_op jit(solution)/shard_map/all_gather | solution.py:25
  175.9 3.9 %fusion.15 = (f32[1,16,96,256]{3,2,0,1:T(8,128)}, f32[1,16,96,256]{3,2,0,1:T(8,128)}) fusion(f32[2,16,96,256]{3,2,0,1:T(8,128)} %bitcast.12), kind=kLoop, calls=%fused_computation.32 | loop fusion | bytes 6291456 | tf_op jit(solution)/shard_map/slice | solution.py:41
Async XLA Ops:
  7.2 6.1 %copy-start = (bf16[128,1536]{1,0:T(8,128)(2,1)S(1)}, bf16[128,1536]{1,0:T(8,128)(2,1)}, u32[]{:S(2)}) copy-start(bf16[128,1536]{1,0:T(8,128)(2,1)} %param.6) | copy-start | bytes 1179652
  7.2 85.5 %reduce-scatter.3.cloned.1.call-start = ((), (), s32[]{:S(2)}) async-start(), calls=%async_computation.3 | async-start | bytes 3538944 | tf_op jit(solution)/shard_map/reduce_scatter | solution.py:23
  8.7 4.5 %copy-start.1 = (bf16[128,256]{1,0:T(8,128)(2,1)S(1)}, bf16[128,256]{1,0:T(8,128)(2,1)}, u32[]{:S(2)}) copy-start(bf16[128,256]{1,0:T(8,128)(2,1)} %param.7) | copy-start | bytes 196612
  15.5 86.4 %reduce-scatter.5.cloned.1.call-start = ((), (), s32[]{:S(2)}) async-start(), calls=%async_computation.4 | async-start | bytes 589824 | tf_op jit(solution)/shard_map/reduce_scatter | solution.py:24
  92.7 35.0 %all-reduce.2.cloned.1.call-start = ((), (), s32[]{:S(2)}) async-start(), calls=%async_computation.5 | async-start | bytes 393216 | tf_op jit(solution)/shard_map/psum | solution.py:22
  101.9 74.0 %all-gather.3.cloned.1.call-start = ((), (), s32[]{:S(2)}) async-start(), calls=%async_computation.2 | async-start | bytes 3342336 | tf_op jit(solution)/shard_map/all_gather | solution.py:25
Sparse Core Ops, SparseCore 0:
  15.7 77.0 reduce-scatter.2
  94.9 6.8 reduce-scatter.4
  104.2 23.5 all-reduce.1
  130.4 45.4 all-gather.2
